TPU v7x, 32 devices: a whole 2x2x4 slice. The times are simulated.
32 devices in a mesh: grp: 8 (over z, core), head: 4 (over y, x).
Axes of the slice: x: 2, y: 2, z: 4, core: 2. Of those that a mesh axis runs over, the one named last changes fastest.
Arguments:
- hidden: bfloat16 [64, 5376], P('grp'), may hold values from -6 to 6
- pre_gain: float32 [5376], replicated, may hold values from 0.5 to 1.5
- query_weight: bfloat16 [5376, 4096], P(None, 'head'), may hold values from -0.078125 to 0.078125
- key_weight: bfloat16 [5376, 2048], P(None, 'head'), may hold values from -0.078125 to 0.078125
- value_weight: bfloat16 [5376, 2048], P(None, 'head'), may hold values from -0.078125 to 0.078125
- out_weight: bfloat16 [4096, 5376], P('head'), may hold values from -0.09375 to 0.09375
- query_norm_gain: float32 [128], replicated, may hold values from 0.1 to 1.9
- key_gain: float32 [128], replicated, may hold values from 0.1 to 1.9
- post_gain: float32 [5376], P('head'), may hold values from 0.1 to 1.9
- text_keys: bfloat16 [64, 1024, 2048], P('grp', None, 'head'), may hold values from -360 to 360
- text_values: bfloat16 [64, 1024, 2048], P('grp', None, 'head'), may hold values from -6 to 6
- text_position: int32 [64], P('grp'), may hold values from 1 to 4095
- image_keys: bfloat16 [192, 256, 2048], P('grp', None, 'head'), may hold values from -360 to 360
- image_values: bfloat16 [192, 256, 2048], P('grp', None, 'head'), may hold values from -6 to 6
- image_owner: int32 [64], replicated, may hold values from 0 to 7, as said below
- image_slot: int32 [64], replicated, may hold values from 0 to 23, as said below
- image_count: int32 [64], replicated, may hold values from 128 to 256, as said below
Outputs:
- updated: bfloat16 [64, 5376], P('grp', 'head')
Inputs may be any that keep to these rules, and one draw needn't show every extreme that they name: `image_owner`: each group owns at most 24 requests, and some group owns exactly 24. `image_slot`: requests with the same owner have distinct slots. `image_count`: A multiple of 128.
All inputs are finite; a program needn't handle non-finite values.
Results may differ from a plain program's by a relative error of at most 0.0055.
The roundings to bfloat16 on the way count: a program that leaves them out, or rounds other values in their place, can miss the bound.
Values may be sent and summed in bfloat16 or wider, within the bound.
No kernel may reach another device: no remote copies, remote signals or barrier semaphores. Data moves between devices by JAX's collectives and lax.ppermute only.
A program may use at most 192 MiB of HBM per device.

v0:
```python
import functools
import math

import jax
import jax.numpy as jnp
from jax import lax
from jax.experimental import pallas as pl
from jax.experimental.pallas import tpu as pltpu
from jax.sharding import PartitionSpec as P


EPS = 1e-06
NEG = -1e30
SMALL = 4 << 20
F32 = jnp.float32
BF16 = jnp.bfloat16
HBM = pl.BlockSpec(memory_space=pltpu.HBM)
VMEM = pl.BlockSpec(memory_space=pltpu.VMEM)
SMEM = pl.BlockSpec(memory_space=pltpu.SMEM)


def cost(flops, nbytes):
    return pl.CostEstimate(flops=flops, bytes_accessed=nbytes, transcendentals=0)


def pieces_of(rows, most):
    for size in range(most, 0, -16):
        if rows % size == 0:
            return size
    return rows


def row_copies(src, dst, sems, size):
    return [
        pltpu.make_async_copy(
            src.at[pl.ds(i * size, size)], dst.at[pl.ds(i * size, size)], sems.at[i]
        )
        for i in range(src.shape[0] // size)
    ]


def rms_rope(v, gain, cosine, sine):
    mean_sq = jnp.mean(v * v, axis=-1, keepdims=True)
    v = v * lax.rsqrt(mean_sq + EPS) * gain
    return v * cosine + pltpu.roll(v, v.shape[-1] // 2, 1) * sine


def query_kernel(
    scale, size, freq, hidden, gain, q_gain_in, k_gain, position_in, owner, count, slot, weight,
    q_out, normed_out, cos_out, sin_out, k_gain_out, position, owner_out, count_out, slot_out,
    w_buf, h_buf, g_buf, q_gain, heads_buf, w_sem, s_sem
):
    copies = row_copies(weight, w_buf, w_sem, size)
    pairs = (
        (hidden, h_buf), (gain, g_buf), (position_in, position), (q_gain_in, q_gain),
        (k_gain, k_gain_out), (owner, owner_out), (count, count_out), (slot, slot_out),
    )
    small = [pltpu.make_async_copy(a, b, s_sem.at[i]) for i, (a, b) in enumerate(pairs)]
    for c in small[:2] + copies[:1] + small[2:] + copies[1:]:
        c.start()
    rows = hidden.shape[0]
    dim = q_gain.shape[-1]
    for c in small[:2]:
        c.wait()
    h = h_buf[...].astype(F32)
    mean_sq = jnp.mean(h * h, axis=-1, keepdims=True)
    h = h * lax.rsqrt(mean_sq + EPS)
    for n in range(g_buf.shape[0]):
        part = slice(n * dim, (n + 1) * dim)
        normed_out[:, part] = (h[:, part] * g_buf[n : n + 1, :]).astype(BF16)
    acc = jnp.zeros((rows, weight.shape[1]), F32)
    for i, c in enumerate(copies):
        c.wait()
        acc = acc + jnp.dot(
            normed_out[:, i * size : (i + 1) * size],
            w_buf[i * size : (i + 1) * size, :],
            preferred_element_type=F32,
        )
        if i == 0:
            small[2].wait()
            lane = lax.broadcasted_iota(jnp.int32, (rows, dim), 1)
            row = lax.broadcasted_iota(jnp.int32, (rows, dim), 0)
            where = jnp.zeros((rows, dim), jnp.int32)
            for n in range(rows):
                where = jnp.where(row == n, position[n], where)
            angle = where.astype(F32) * freq[...]
            cosine = jnp.cos(angle)
            sine = jnp.sin(angle)
            sine = jnp.where(lane < dim // 2, -sine, sine)
            cos_out[...] = cosine
            sin_out[...] = sine
    for c in small[3:]:
        c.wait()
    cosine, sine = cos_out[...], sin_out[...]
    for n in range(acc.shape[1] // dim):
        v = rms_rope(acc[:, n * dim : (n + 1) * dim], q_gain[...], cosine, sine)
        heads_buf[:, n, :] = v * scale
    q_out[...] = heads_buf[...].astype(BF16)


def kv_kernel(normed, cosine, sine, k_gain, q, k_weight, v_weight, self_out, v_out, heads_buf):
    k_acc = jnp.dot(normed[...], k_weight[...], preferred_element_type=F32)
    v_acc = jnp.dot(normed[...], v_weight[...], preferred_element_type=F32)
    dim = k_gain.shape[-1]
    heads = q.shape[1]
    group = heads // (k_acc.shape[1] // dim)
    for n in range(heads):
        if n % group == 0:
            part = slice((n // group) * dim, (n // group + 1) * dim)
            k = rms_rope(k_acc[:, part], k_gain[...], cosine[...], sine[...])
            k = k.astype(BF16).astype(F32)
            v = v_acc[:, part].astype(BF16).astype(F32)
        heads_buf[:, n, :] = k
        v_out[:, n, :] = v
    score = jnp.sum(q[...].astype(F32) * heads_buf[...], axis=-1, keepdims=True)
    self_out[...] = jnp.broadcast_to(score, self_out.shape)


def text_parts(rows):
    return ((0, rows // 2), (rows // 2, rows))


def spread(q, kv_heads):
    group = q.shape[0] // kv_heads
    owner = lax.broadcasted_iota(jnp.int32, q.shape, 0) // group
    q = q.astype(F32)
    return jnp.concatenate(
        [jnp.where(owner == n, q, 0.0) for n in range(kv_heads)], axis=1
    ).astype(BF16)


def gather_heads(o, heads, dim):
    kv_heads = o.shape[1] // dim
    owner = lax.broadcasted_iota(jnp.int32, (heads, dim), 0) // (heads // kv_heads)
    total = jnp.zeros((heads, dim), F32)
    for n in range(kv_heads):
        total = jnp.where(owner == n, o[:, n * dim : (n + 1) * dim], total)
    return total


def score_block(q, keys, valid):
    scores = lax.dot_general(
        spread(q, keys.shape[1] // q.shape[1]), keys, (((1,), (1,)), ((), ())),
        preferred_element_type=F32,
    )
    return jnp.where(valid, scores, NEG)


def weigh_block(scores, values, heads, dim):
    top = jnp.max(scores, axis=-1, keepdims=True)
    weights = jnp.exp(scores - top).astype(BF16)
    total = jnp.sum(weights.astype(F32), axis=-1, keepdims=True)
    summed = jnp.dot(weights, values, preferred_element_type=F32)
    return top, total, gather_heads(summed, heads, dim)


def plan(slots, owner, count, slot, item, length, filled):
    me = lax.axis_index("grp")

    def note(r, have):
        hit = owner[r] == me
        at = jnp.where(hit, have, slots)
        item[at] = r * slots + slot[r]
        length[at] = count[r]
        return have + hit.astype(jnp.int32)

    filled[0] = lax.fori_loop(0, owner.shape[0], note, jnp.int32(0), unroll=8)


def text_kernel(first, slots, position, q, *refs):
    if slots:
        owner, count_in, slot_in = refs[:3]
        keys, values, o_out, m_out, l_out, item, length, filled = refs[3:11]
        k_buf, v_buf, k_sem, v_sem = refs[11:]
    else:
        keys, values, o_out, m_out, l_out, k_buf, v_buf, k_sem, v_sem = refs
    count, window, _ = k_buf.shape
    heads, dim = q.shape[1:]
    copies = [
        [
            pltpu.make_async_copy(src.at[first + i], dst.at[i], sem.at[i])
            for src, dst, sem in ((keys, k_buf, k_sem), (values, v_buf, v_sem))
        ]
        for i in range(count)
    ]
    for pair in copies:
        for c in pair:
            c.start()
    if slots:
        plan(slots, owner, count_in, slot_in, item, length, filled)
    column = lax.broadcasted_iota(jnp.int32, (heads, window), 1)

    def score(i):
        p = position[first + i]
        valid = (column < p) & (column != lax.rem(p, window))
        return score_block(q[first + i], k_buf[i], valid)

    copies[0][0].wait()
    scores = score(0)
    for i in range(count):
        if i + 1 < count:
            copies[i + 1][0].wait()
        copies[i][1].wait()
        later = score(i + 1) if i + 1 < count else None
        top, total, summed = weigh_block(scores, v_buf[i], heads, dim)
        o_out[i] = summed
        m_out[i] = jnp.broadcast_to(top, summed.shape)
        l_out[i] = jnp.broadcast_to(total, summed.shape)
        scores = later


def image_kernel(batch, n_q, item, tokens, filled, *refs):
    queries = refs[:n_q]
    keys, values, mine, other, q_buf, s_buf, out_buf = refs[n_q:]
    me = lax.axis_index("grp")
    slots, length, _ = keys.shape
    rows = queries[0].shape[0]
    heads, dim = queries[0].shape[1:]
    half = mine.shape[0]
    have = filled[0]
    out_buf[...] = jnp.zeros_like(out_buf)
    known, step = [0], half
    q_buf[:rows] = queries[0][...]
    for ref in queries[1:]:
        new = [j ^ step for j in known]
        step //= 2
        for n, j in enumerate(new):
            q_buf[j * rows : (j + 1) * rows] = ref[n * rows : (n + 1) * rows]
        known = known + new
    column = lax.broadcasted_iota(jnp.int32, (heads, length), 1)
    lane_of = lax.broadcasted_iota(jnp.int32, (heads, dim), 1)

    def members(t):
        found = []
        for u in range(batch):
            n = t * batch + u
            live = n < have
            n = jnp.minimum(n, have - 1)
            r = item[n] // slots
            found.append((n, live, r, item[n] - r * slots))
        return found

    def score(t):
        for u, (n, live, r, place) in enumerate(members(t)):
            group, lane = lax.bitwise_xor(r // rows, me), lax.rem(r, rows)
            s_buf[lax.rem(t, 2), u] = score_block(
                q_buf[group * rows + lane], keys[place], column < tokens[n]
            )

    def weigh(t):
        done = []
        for u, (n, live, r, place) in enumerate(members(t)):
            top, total, summed = weigh_block(s_buf[lax.rem(t, 2), u], values[place], heads, dim)
            mean = (summed / total).astype(BF16)
            group, lane = lax.bitwise_xor(r // rows, me), lax.rem(r, rows)
            level = top + jnp.log(total)
            high = level.astype(BF16).astype(F32)
            middle = (level - high).astype(BF16).astype(F32)
            low = level - high - middle
            kind = lane_of - 3 * lane
            stats = jnp.where(
                kind == 0, high, jnp.where(kind == 1, middle, jnp.where(kind == 2, low, 0.0))
            )
            at = jnp.where(live, group, 2 * half) * (rows + 1)
            done.append((at + lane, at + rows, mean, stats))
        for at, stats_at, mean, stats in done:
            out_buf[at] = mean
            out_buf[stats_at] = (out_buf[stats_at].astype(F32) + stats).astype(BF16)

    last = (have + batch - 1) // batch - 1

    @pl.when(have > 0)
    def _():
        score(0)

        def both(t, carry):
            score(t + 1)
            weigh(t)
            return carry

        lax.fori_loop(0, last, both, 0)
        weigh(last)

    for j in range(half):
        for n in range(rows + 1):
            mine[j, n] = out_buf[2 * j * (rows + 1) + n]
            other[j, n] = out_buf[(2 * j + 1) * (rows + 1) + n]


def out_kernel(size, n_image, n_text, *refs):
    images = refs[:n_image]
    text = refs[n_image : n_image + n_text]
    own, v_new, weight, sent, kept, heads_buf, at_buf = refs[n_image + n_text :]
    rows, heads, dim = own.shape
    holds = [(n, i) for n in range(0, n_text, 3) for i in range(text[n].shape[0])]
    stats = images[0][rows].astype(F32)
    for ref in images[1:]:
        stats = stats + ref[rows].astype(F32)
    for r in range(rows):
        mean = images[0][r].astype(F32)
        for ref in images[1:]:
            mean = mean + ref[r].astype(F32)
        image_level = (
            stats[:, 3 * r : 3 * r + 1] + stats[:, 3 * r + 1 : 3 * r + 2]
        ) + stats[:, 3 * r + 2 : 3 * r + 3]
        part, at = holds[r]
        o_text, m, l_text = (ref[at] for ref in text[part : part + 3])
        s = own[r]
        top = jnp.maximum(jnp.maximum(image_level, m), s)
        e_image = jnp.exp(image_level - top)
        e_text = jnp.exp(m - top)
        e_own = jnp.exp(s - top)
        upper = mean * e_image + o_text * e_text + v_new[r] * e_own
        lower = e_image + l_text * e_text + e_own
        heads_buf[r] = upper / lower
    for n in range(heads):
        at_buf[:, n * dim : (n + 1) * dim] = heads_buf[:, n, :].astype(BF16)
    for i in range(weight.shape[0] // size):
        part = jnp.dot(
            at_buf[:, i * size : (i + 1) * size],
            weight[i * size : (i + 1) * size, :],
            preferred_element_type=F32,
        )
        if i == 0:
            kept[...] = part
        else:
            kept[...] += part
    sent[...] = kept[...].astype(BF16)


def final_kernel(n_others, *refs):
    others = refs[:n_others]
    kept, hidden, gain, out = refs[n_others:]
    y = kept[...]
    for ref in others:
        y = y + ref[...].astype(F32)
    mean_sq = jnp.sum(y * y, axis=-1, keepdims=True) / y.shape[1]
    scale = lax.rsqrt(mean_sq + EPS)
    width = out.shape[1]
    me = lax.axis_index("head")
    for n in range(y.shape[1] // width):
        @pl.when(me == n)
        def _():
            part = slice(n * width, (n + 1) * width)
            out[...] = (hidden[:, part].astype(F32) + y[:, part] * scale * gain[...]).astype(BF16)


def stay(x):
    return pltpu.with_memory_space_constraint(x, pltpu.HBM)


def swap(x, axis, k):
    n = lax.axis_size(axis)
    return lax.ppermute(x, axis, [(i, i ^ k) for i in range(n)])


def body(
    hidden, pre_gain, query_weight, key_weight, value_weight, out_weight, query_norm_gain, key_gain,
    post_gain, text_keys, text_values, text_position, image_keys, image_values, image_owner,
    image_slot, image_count,
):
    rows, width = hidden.shape
    dim = query_norm_gain.shape[0]
    heads = query_weight.shape[1] // dim
    groups = lax.axis_size("grp")
    head_parts = lax.axis_size("head")
    slots, length = image_keys.shape[0], image_keys.shape[1]
    scale = 1.0 / math.sqrt(width // (heads * head_parts))
    half = dim // 2
    freq = jnp.exp(-jnp.log(1000000.0) * jnp.arange(half, dtype=F32) / half)
    freq = jnp.concatenate([freq, freq])[None, :]

    size = pieces_of(width, 768)
    n_copies = width // size
    whole = jax.ShapeDtypeStruct(image_owner.shape, jnp.int32)
    q, normed, cosine, sine, k_gain, position, owner, count, slot = pl.pallas_call(
        functools.partial(query_kernel, scale, size),
        out_shape=(
            jax.ShapeDtypeStruct((rows, heads, dim), BF16),
            jax.ShapeDtypeStruct((rows, width), BF16),
            jax.ShapeDtypeStruct((rows, dim), F32),
            jax.ShapeDtypeStruct((rows, dim), F32),
            jax.ShapeDtypeStruct((1, dim), F32),
            jax.ShapeDtypeStruct((rows,), jnp.int32),
            whole, whole, whole,
        ),
        in_specs=[VMEM] + [HBM] * 9,
        out_specs=(VMEM,) * 5 + (SMEM,) * 4,
        scratch_shapes=[
            pltpu.VMEM(query_weight.shape, BF16),
            pltpu.VMEM(hidden.shape, BF16),
            pltpu.VMEM((width // dim, dim), F32),
            pltpu.VMEM((1, dim), F32),
            pltpu.VMEM((rows, heads, dim), F32),
            pltpu.SemaphoreType.DMA((n_copies,)),
            pltpu.SemaphoreType.DMA((8,)),
        ],
        compiler_params=pltpu.CompilerParams(vmem_limit_bytes=16 << 20),
        cost_estimate=cost(2 * rows * query_weight.size, 2 * query_weight.size),
        name="query",
    )(
        freq,
        *map(
            stay,
            (
                hidden, pre_gain.reshape(-1, dim), query_norm_gain.reshape(1, -1),
                key_gain.reshape(1, -1), text_position, image_owner, image_count, image_slot,
                query_weight,
            ),
        ),
    )

    queries = [q]
    held = q
    k = groups // 2
    while k:
        got = swap(held, "grp", k)
        queries.append(got)
        k //= 2
        if k:
            held = jnp.concatenate([held, got], axis=0)

    text = []
    for n, (first, last) in enumerate(text_parts(rows)):
        part = (last - first,) + text_keys.shape[1:]
        share = math.prod(part)
        lead = n == 0
        got = pl.pallas_call(
            functools.partial(text_kernel, first, slots if lead else 0),
            out_shape=(jax.ShapeDtypeStruct((last - first, heads, dim), F32),) * 3
            + lead * (
                jax.ShapeDtypeStruct((slots + 1,), jnp.int32),
                jax.ShapeDtypeStruct((slots + 1,), jnp.int32),
                jax.ShapeDtypeStruct((1,), jnp.int32),
            ),
            in_specs=[SMEM, VMEM] + lead * [SMEM] * 3 + [HBM, HBM],
            out_specs=(VMEM,) * 3 + lead * (SMEM,) * 3,
            scratch_shapes=[
                pltpu.VMEM(part, BF16),
                pltpu.VMEM(part, BF16),
                pltpu.SemaphoreType.DMA(part[:1]),
                pltpu.SemaphoreType.DMA(part[:1]),
            ],
            compiler_params=pltpu.CompilerParams(vmem_limit_bytes=4 * share + SMALL),
            cost_estimate=cost(8 * heads * share, 4 * share),
        )(position, q, *(lead * (owner, count, slot)), stay(text_keys), stay(text_values))
        text += got[:3]
        if lead:
            items = got[3:]

    batch = 8
    mine, other = pl.pallas_call(
        functools.partial(image_kernel, batch, len(queries)),
        out_shape=(jax.ShapeDtypeStruct((groups // 2, rows + 1, heads, dim), BF16),) * 2,
        in_specs=[SMEM] * 3 + [VMEM] * (len(queries) + 2),
        out_specs=(VMEM, VMEM),
        scratch_shapes=[
            pltpu.VMEM((groups * rows, heads, dim), BF16),
            pltpu.VMEM((2, batch, heads, length), F32),
            pltpu.VMEM(((groups + 1) * (rows + 1), heads, dim), BF16),
        ],
        compiler_params=pltpu.CompilerParams(vmem_limit_bytes=SMALL),
        cost_estimate=cost(8 * heads * image_keys.size, 4 * image_keys.size),
        name="image",
    )(*items, *queries, image_keys, image_values)

    key_weight, value_weight, out_weight, mine, other = lax.optimization_barrier(
        (key_weight, value_weight, out_weight, mine, other)
    )
    own_score, v_new = pl.pallas_call(
        kv_kernel,
        out_shape=(jax.ShapeDtypeStruct((rows, heads, dim), F32),) * 2,
        in_specs=[VMEM] * 7,
        out_specs=(VMEM, VMEM),
        scratch_shapes=[pltpu.VMEM((rows, heads, dim), F32)],
        compiler_params=pltpu.CompilerParams(vmem_limit_bytes=SMALL),
        cost_estimate=cost(4 * rows * key_weight.size, 4 * key_weight.size),
        name="keyvalue",
    )(normed, cosine, sine, k_gain, q, key_weight, value_weight)

    got = swap(other, "grp", 1)
    images = []
    for j in range(groups // 2):
        moved = mine[j] + got[j]
        images.append(swap(moved, "grp", 2 * j) if j else moved)

    o_size = pieces_of(out_weight.shape[0], 256)
    sent, kept = pl.pallas_call(
        functools.partial(out_kernel, o_size, len(images), len(text)),
        out_shape=(
            jax.ShapeDtypeStruct((rows, width), BF16),
            jax.ShapeDtypeStruct((rows, width), F32),
        ),
        in_specs=[VMEM] * (len(images) + len(text) + 3),
        out_specs=(VMEM, VMEM),
        scratch_shapes=[pltpu.VMEM((rows, heads, dim), F32), pltpu.VMEM((rows, heads * dim), BF16)],
        compiler_params=pltpu.CompilerParams(vmem_limit_bytes=SMALL),
        cost_estimate=cost(2 * rows * out_weight.size, 2 * out_weight.size),
        name="project",
    )(*images, *text, own_score, v_new, out_weight)

    others = [swap(sent, "head", j) for j in range(1, head_parts)]
    return pl.pallas_call(
        functools.partial(final_kernel, len(others)),
        out_shape=jax.ShapeDtypeStruct((rows, width // head_parts), BF16),
        in_specs=[VMEM] * (len(others) + 3),
        out_specs=VMEM,
        compiler_params=pltpu.CompilerParams(vmem_limit_bytes=SMALL),
        cost_estimate=cost(8 * rows * width, 16 * rows * width),
        name="finish",
    )(*others, kept, hidden, post_gain.reshape(1, -1))


def solution(mesh):
    placed = (
        P("grp", None),
        P(),
        P(None, "head"),
        P(None, "head"),
        P(None, "head"),
        P("head", None),
        P(),
        P(),
        P("head"),
        P("grp", None, "head"),
        P("grp", None, "head"),
        P("grp"),
        P("grp", None, "head"),
        P("grp", None, "head"),
        P(),
        P(),
        P(),
    )
    return jax.shard_map(
        body, mesh=mesh, in_specs=placed, out_specs=P("grp", "head"), check_vma=False
    )
```

profile of v0, /device:TPU:0, one launch (start us, length us, event | category | flops | bytes accessed | tf_op | source)
XLA Modules:
  0.0 50.1 jit_solution(2386904246895347853)
XLA Ops:
  0.0 0.1 maximum_bitcast_fusion.freq
  0.1 0.0 slice-start.3
  0.1 0.0 slice-start.5
  0.1 5.5 %query.1 = (bf16[8,8,128]{2,1,0:T(8,128)(2,1)S(1)}, bf16[8,5376]{1,0:T(8,128)(2,1)S(1)}, f32[8,128]{1,0:T(8,128)S(1)}, f32[8,128]{1,0:T(8,128)S(1)}, f32[1,128]{...) custom-call(f32[1,128]{1,0:T(1,128)S(1)} %maximum_bitcast_fusion.freq, ...), custom_call_target="tpu_custom_call" | custom-call | flops 88080384 | bytes 11010048 | tf_op jit(solution)/shard_map/query/pallas_call | solution.py:376
  5.6 4.1 %collective-permute-start = (bf16[8,8,128]{2,1,0:T(8,128)(2,1)S(1)}, bf16[8,8,128]{2,1,0:T(8,128)(2,1)S(1)}, u32[]{:S(2)}, u32[]{:S(2)}) collective-permute-start(bf16[8,8,128]{2,1,0:T(8,128)(2,1)S(1)} %get-tuple-element.35.q.refs_0_), channel_id=1, source_target_pairs={{0,16},{4,20},{8,24},{12,28},{16,0},{20,4},{24,8},{28,12},{1,17},{... | collective-permute-start | bytes 49160 | tf_op jit(solution)/shard_map/ppermute | solution.py:354
  9.7 1.7 %collective-permute-done.refs_1_ = bf16[8,8,128]{2,1,0:T(8,128)(2,1)S(1)} collective-permute-done((bf16[8,8,128]{2,1,0:T(8,128)(2,1)S(1)}, bf16[8,8,128]{2,1,0:T(8,128)(2,1)S(1)}, u32[]{:S(2)}, u32[]{:S(2)}) %collective-permute-start) | collective-permute-done | bytes 16416 | tf_op jit(solution)/shard_map/ppermute | solution.py:354
  11.4 1.9 %collective-permute-start.1 = (bf16[16,8,128]{2,1,0:T(8,128)(2,1)S(1)}, bf16[16,8,128]{2,1,0:T(8,128)(2,1)S(1)}, u32[]{:S(2)}, u32[]{:S(2)}) collective-permute-start(bf16[16,8,128]{2,1,0:T(8,128)(2,1)S(1)} %pad_maximum_fusion.1), channel_id=1, source_target_pairs={{0,8},{4,12},{8,0},{12,4},{16,24},{20,28},{24,16},{28,20},{1,9},{5... | collective-permute-start | bytes 98312 | tf_op jit(solution)/shard_map/ppermute | solution.py:354
  13.4 2.0 %collective-permute-done.1.refs_2_ = bf16[16,8,128]{2,1,0:T(8,128)(2,1)S(1)} collective-permute-done((bf16[16,8,128]{2,1,0:T(8,128)(2,1)S(1)}, bf16[16,8,128]{2,1,0:T(8,128)(2,1)S(1)}, u32[]{:S(2)}, u32[]{:S(2)}) %collective-permute-start.1) | collective-permute-done | bytes 32800 | tf_op jit(solution)/shard_map/ppermute | solution.py:354
  15.4 0.1 collective-permute-start.2
  15.5 0.0 slice-start.4
  15.5 0.0 slice-start.6
  15.5 5.2 %shard_map.163 = (f32[4,8,128]{2,1,0:T(8,128)S(1)}, f32[4,8,128]{2,1,0:T(8,128)S(1)}, f32[4,8,128]{2,1,0:T(8,128)S(1)}, s32[25]{0:T(128)S(1)}, s32[25]{0:T(128)S(1)}, /*index=5*/s32[1]{0:T(128)}) custom-call(s32[8]{0:T(128)S(1)} %get-tuple-element.34.position, bf16[8,8,128]{2,1,0:T(8,128)(2,1)S(1)} %get-tuple-element.35.q.refs_0_, ...), custom_call_target="tpu_custom_call" | custom-call | flops 134217728 | bytes 8388608 | tf_op jit(solution)/shard_map/pallas_call | solution.py:428
  20.7 0.0 collective-permute-done.2.refs_3_
  20.7 0.0 slice-done.3
  20.7 0.0 slice-done.5
  20.7 0.0 slice-done.4
  20.7 0.0 slice-done.6
  20.7 2.4 %image.1 = (bf16[4,9,8,128]{3,2,1,0:T(8,128)(2,1)S(1)}, bf16[4,9,8,128]{3,2,1,0:T(8,128)(2,1)S(1)}) custom-call(s32[25]{0:T(128)S(1)} %get-tuple-element.39.item, s32[25]{0:T(128)S(1)} %get-tuple-element.40.tokens, s32[1]{0:T(128)} %get-tuple-element.41.filled, bf16[8,8,128]{2,1,0:T(8,128)(2,1)S(1)} %get-tuple-element.35.q.refs_0_, ...), custom_call_target="tpu_custom_call" | custom-call | flops 201326592 | bytes 12582912 | tf_op jit(solution)/shard_map/image/pallas_call | solution.py:452
  23.1 2.4 %collective-permute-start.3 = (bf16[4,9,8,128]{3,2,1,0:T(8,128)(2,1)S(1)}, bf16[4,9,8,128]{3,2,1,0:T(8,128)(2,1)S(1)}, u32[]{:S(2)}, u32[]{:S(2)}) collective-permute-start(bf16[4,9,8,128]{3,2,1,0:T(8,128)(2,1)S(1)} %get-tuple-element.45), channel_id=1, source_target_pairs={{0,4},{4,0},{8,12},{12,8},{16,20},{20,16},{24,28},{28,24},{1,5},{5... | collective-permute-start | bytes 221192 | tf_op jit(solution)/shard_map/ppermute | solution.py:354
  25.5 0.9 %collective-permute-done.3 = bf16[4,9,8,128]{3,2,1,0:T(8,128)(2,1)S(1)} collective-permute-done((bf16[4,9,8,128]{3,2,1,0:T(8,128)(2,1)S(1)}, bf16[4,9,8,128]{3,2,1,0:T(8,128)(2,1)S(1)}, u32[]{:S(2)}, u32[]{:S(2)}) %collective-permute-start.3) | collective-permute-done | bytes 73760 | tf_op jit(solution)/shard_map/ppermute | solution.py:354
  26.4 0.1 collective-permute-start.4
  26.5 2.7 %collective-permute-start.5 = (bf16[9,8,128]{2,1,0:T(8,128)(2,1)S(1)}, bf16[9,8,128]{2,1,0:T(8,128)(2,1)S(1)}, u32[]{:S(2)}, u32[]{:S(2)}) collective-permute-start(bf16[9,8,128]{2,1,0:T(8,128)(2,1)S(1)} %get-tuple-element.64), channel_id=1, source_target_pairs={{0,16},{4,20},{8,24},{12,28},{16,0},{20,4},{24,8},{28,12},{1,17},{... | collective-permute-start | bytes 55304 | tf_op jit(solution)/shard_map/ppermute | solution.py:354
  29.2 0.0 slice-start.7
  29.2 0.0 slice-start.9
  29.2 0.0 slice-start.8
  29.2 0.0 slice-start.10
  29.2 1.8 %collective-permute-start.6 = (bf16[9,8,128]{2,1,0:T(8,128)(2,1)S(1)}, bf16[9,8,128]{2,1,0:T(8,128)(2,1)S(1)}, u32[]{:S(2)}, u32[]{:S(2)}) collective-permute-start(bf16[9,8,128]{2,1,0:T(8,128)(2,1)S(1)} %get-tuple-element.63), channel_id=1, source_target_pairs={{0,24},{4,28},{8,16},{12,20},{16,8},{20,12},{24,0},{28,4},{1,25},{... | collective-permute-start | bytes 55304 | tf_op jit(solution)/shard_map/ppermute | solution.py:354
  31.0 0.0 slice-start
  31.0 0.0 slice-start.1
  31.0 5.3 %shard_map.164 = (f32[4,8,128]{2,1,0:T(8,128)S(1)}, f32[4,8,128]{2,1,0:T(8,128)S(1)}, f32[4,8,128]{2,1,0:T(8,128)S(1)}) custom-call(s32[8]{0:T(128)S(1)} %get-tuple-element.34.position, bf16[8,8,128]{2,1,0:T(8,128)(2,1)S(1)} %get-tuple-element.35.q.refs_0_, bf16[8,1024,512]{2,1,0:T(8,128)(2,1)} %refs_0_.1, bf16[8,1024,512]{2,1,0:T(8,128)(2,1)} %refs_1_.1), custom_call_target="tpu_custom_call" | custom-call | flops 134217728 | bytes 8388608 | tf_op jit(solution)/shard_map/pallas_call | solution.py:428
  36.3 0.0 slice-done.7
  36.3 0.0 slice-done.9
  36.3 0.0 slice-done.8
  36.3 0.0 slice-done.10
  36.3 0.0 slice-start.2
  36.3 1.6 %keyvalue.1 = (f32[8,8,128]{2,1,0:T(8,128)S(1)}, f32[8,8,128]{2,1,0:T(8,128)S(1)}) custom-call(bf16[8,5376]{1,0:T(8,128)(2,1)S(1)} %get-tuple-element.52.normed, f32[8,128]{1,0:T(8,128)S(1)} %get-tuple-element.53.cosine, f32[8,128]{1,0:T(8,128)S(1)} %get-tuple-element.54.sine, f32[1,128]{1,0:T(1,128)S(1)} %get-tuple-element.55.k_gain, ...), custom_call_target="tpu_custom_call" | custom-call | flops 88080384 | bytes 11010048 | tf_op jit(solution)/shard_map/keyvalue/pallas_call | solution.py:470
  37.9 0.0 copy-start.1
  37.9 0.0 copy-start
  37.9 0.0 collective-permute-done.4.refs_1_
  38.0 0.0 collective-permute-done.5.refs_2_
  38.0 0.0 collective-permute-done.6.refs_3_
  38.0 0.0 slice-done
  38.0 0.5 slice-done.1
  38.4 0.8 %slice-done.2 = s8[2621440]{0:T(1024)(128)(4,1)S(1)} async-done(((s8[11010048]{0:T(1024)(128)(4,1)}), s8[2621440]{0:T(1024)(128)(4,1)S(1)}, s32[]{:S(2)}) %slice-start.2) | async-done | bytes 2621464
  39.2 1.7 %project.1 = (bf16[8,5376]{1,0:T(8,128)(2,1)S(1)}, f32[8,5376]{1,0:T(8,128)S(1)}) custom-call(bf16[9,8,128]{2,1,0:T(8,128)(2,1)S(1)} %get-tuple-element.66.refs_0_, bf16[9,8,128]{2,1,0:T(8,128)(2,1)S(1)} %collective-permute-done.4.refs_1_, bf16[9,8,128]{2,1,0:T(8,128)(2,1)S(1)} %collective-permute-done.5.refs_2_, ...), custom_call_target="tpu_custom_call" | custom-call | flops 88080384 | bytes 11010048 | tf_op jit(solution)/shard_map/project/pallas_call | solution.py:488
  40.9 1.5 %collective-permute-start.7 = (bf16[8,5376]{1,0:T(8,128)(2,1)S(1)}, bf16[8,5376]{1,0:T(8,128)(2,1)S(1)}, u32[]{:S(2)}, u32[]{:S(2)}) collective-permute-start(bf16[8,5376]{1,0:T(8,128)(2,1)S(1)} %get-tuple-element.61), channel_id=1, source_target_pairs={{0,1},{1,0},{2,3},{3,2},{4,5},{5,4},{6,7},{7,6},{8,9},{9,8},{10,11... | collective-permute-start | bytes 258056 | tf_op jit(solution)/shard_map/ppermute | solution.py:354
  42.4 1.5 %collective-permute-start.8 = (bf16[8,5376]{1,0:T(8,128)(2,1)S(1)}, bf16[8,5376]{1,0:T(8,128)(2,1)S(1)}, u32[]{:S(2)}, u32[]{:S(2)}) collective-permute-start(bf16[8,5376]{1,0:T(8,128)(2,1)S(1)} %get-tuple-element.61), channel_id=1, source_target_pairs={{0,2},{1,3},{2,0},{3,1},{4,6},{5,7},{6,4},{7,5},{8,10},{9,11},{10,... | collective-permute-start | bytes 258056 | tf_op jit(solution)/shard_map/ppermute | solution.py:354
  43.9 0.5 collective-permute-start.9
  44.4 0.0 copy-done.1
  44.4 1.0 %collective-permute-done.7.refs_0_ = bf16[8,5376]{1,0:T(8,128)(2,1)S(1)} collective-permute-done((bf16[8,5376]{1,0:T(8,128)(2,1)S(1)}, bf16[8,5376]{1,0:T(8,128)(2,1)S(1)}, u32[]{:S(2)}, u32[]{:S(2)}) %collective-permute-start.7) | collective-permute-done | bytes 86048 | tf_op jit(solution)/shard_map/ppermute | solution.py:354
  45.4 2.4 %collective-permute-done.8.refs_1_ = bf16[8,5376]{1,0:T(8,128)(2,1)S(1)} collective-permute-done((bf16[8,5376]{1,0:T(8,128)(2,1)S(1)}, bf16[8,5376]{1,0:T(8,128)(2,1)S(1)}, u32[]{:S(2)}, u32[]{:S(2)}) %collective-permute-start.8) | collective-permute-done | bytes 86048 | tf_op jit(solution)/shard_map/ppermute | solution.py:354
  47.8 1.5 %collective-permute-done.9.refs_2_ = bf16[8,5376]{1,0:T(8,128)(2,1)S(1)} collective-permute-done((bf16[8,5376]{1,0:T(8,128)(2,1)S(1)}, bf16[8,5376]{1,0:T(8,128)(2,1)S(1)}, u32[]{:S(2)}, u32[]{:S(2)}) %collective-permute-start.9) | collective-permute-done | bytes 86048 | tf_op jit(solution)/shard_map/ppermute | solution.py:354
  49.3 0.0 copy-done
  49.3 0.8 %finish.1 = bf16[8,1344]{1,0:T(8,128)(2,1)} custom-call(bf16[8,5376]{1,0:T(8,128)(2,1)S(1)} %collective-permute-done.7.refs_0_, bf16[8,5376]{1,0:T(8,128)(2,1)S(1)} %collective-permute-done.8.refs_1_, bf16[8,5376]{1,0:T(8,128)(2,1)S(1)} %collective-permute-done.9.refs_2_, f32[8,5376]{1,0:T(8,128)S(1)} %get-tuple-element.62.refs_3_, ...), custom_call_target="tpu_custom_call" | custom-call | flops 344064 | bytes 688128 | tf_op jit(solution)/shard_map/finish/pallas_call | solution.py:503
  (10 shorter events, 0.1 us)
Async XLA Ops:
  0.1 20.6 %slice-start.3 = ((s8[6291456]{0:T(1024)(128)(4,1)}), s8[4194304]{0:T(1024)(128)(4,1)S(1)}, s32[]{:S(2)}) async-start(s8[6291456]{0:T(1024)(128)(4,1)} %bitcast.15), calls=%async_computation.3 | async-start | bytes 8388608
  0.1 20.6 %slice-start.5 = ((s8[6291456]{0:T(1024)(128)(4,1)}), s8[4194304]{0:T(1024)(128)(4,1)S(1)}, s32[]{:S(2)}) async-start(s8[6291456]{0:T(1024)(128)(4,1)} %bitcast.17), calls=%async_computation.5 | async-start | bytes 8388608
  5.6 5.8 %collective-permute-start = (bf16[8,8,128]{2,1,0:T(8,128)(2,1)S(1)}, bf16[8,8,128]{2,1,0:T(8,128)(2,1)S(1)}, u32[]{:S(2)}, u32[]{:S(2)}) collective-permute-start(bf16[8,8,128]{2,1,0:T(8,128)(2,1)S(1)} %get-tuple-element.35.q.refs_0_), channel_id=1, source_target_pairs={{0,16},{4,20},{8,24},{12,28},{16,0},{20,4},{24,8},{28,12},{1,17},{... | collective-permute-start | bytes 49160 | tf_op jit(solution)/shard_map/ppermute | solution.py:354
  11.4 3.9 %collective-permute-start.1 = (bf16[16,8,128]{2,1,0:T(8,128)(2,1)S(1)}, bf16[16,8,128]{2,1,0:T(8,128)(2,1)S(1)}, u32[]{:S(2)}, u32[]{:S(2)}) collective-permute-start(bf16[16,8,128]{2,1,0:T(8,128)(2,1)S(1)} %pad_maximum_fusion.1), channel_id=1, source_target_pairs={{0,8},{4,12},{8,0},{12,4},{16,24},{20,28},{24,16},{28,20},{1,9},{5... | collective-permute-start | bytes 98312 | tf_op jit(solution)/shard_map/ppermute | solution.py:354
  15.4 5.3 %collective-permute-start.2 = (bf16[32,8,128]{2,1,0:T(8,128)(2,1)S(1)}, bf16[32,8,128]{2,1,0:T(8,128)(2,1)S(1)}, u32[]{:S(2)}, u32[]{:S(2)}) collective-permute-start(bf16[32,8,128]{2,1,0:T(8,128)(2,1)S(1)} %pad_maximum_fusion), channel_id=1, source_target_pairs={{0,4},{4,0},{8,12},{12,8},{16,20},{20,16},{24,28},{28,24},{1,5},{5... | collective-permute-start | bytes 196616 | tf_op jit(solution)/shard_map/ppermute | solution.py:354
  15.5 5.2 %slice-start.4 = ((s8[6291456]{0:T(1024)(128)(4,1)}), s8[2097152]{0:T(1024)(128)(4,1)S(1)}, s32[]{:S(2)}) async-start(s8[6291456]{0:T(1024)(128)(4,1)} %bitcast.15), calls=%async_computation.4 | async-start | bytes 4194304
  15.5 5.2 %slice-start.6 = ((s8[6291456]{0:T(1024)(128)(4,1)}), s8[2097152]{0:T(1024)(128)(4,1)S(1)}, s32[]{:S(2)}) async-start(s8[6291456]{0:T(1024)(128)(4,1)} %bitcast.17), calls=%async_computation.6 | async-start | bytes 4194304
  23.1 3.3 %collective-permute-start.3 = (bf16[4,9,8,128]{3,2,1,0:T(8,128)(2,1)S(1)}, bf16[4,9,8,128]{3,2,1,0:T(8,128)(2,1)S(1)}, u32[]{:S(2)}, u32[]{:S(2)}) collective-permute-start(bf16[4,9,8,128]{3,2,1,0:T(8,128)(2,1)S(1)} %get-tuple-element.45), channel_id=1, source_target_pairs={{0,4},{4,0},{8,12},{12,8},{16,20},{20,16},{24,28},{28,24},{1,5},{5... | collective-permute-start | bytes 221192 | tf_op jit(solution)/shard_map/ppermute | solution.py:354
  26.4 11.5 %collective-permute-start.4 = (bf16[9,8,128]{2,1,0:T(8,128)(2,1)S(1)}, bf16[9,8,128]{2,1,0:T(8,128)(2,1)S(1)}, u32[]{:S(2)}, u32[]{:S(2)}) collective-permute-start(bf16[9,8,128]{2,1,0:T(8,128)(2,1)S(1)} %get-tuple-element.65), channel_id=1, source_target_pairs={{0,8},{4,12},{8,0},{12,4},{16,24},{20,28},{24,16},{28,20},{1,9},{5... | collective-permute-start | bytes 55304 | tf_op jit(solution)/shard_map/ppermute | solution.py:354
  26.5 11.4 %collective-permute-start.5 = (bf16[9,8,128]{2,1,0:T(8,128)(2,1)S(1)}, bf16[9,8,128]{2,1,0:T(8,128)(2,1)S(1)}, u32[]{:S(2)}, u32[]{:S(2)}) collective-permute-start(bf16[9,8,128]{2,1,0:T(8,128)(2,1)S(1)} %get-tuple-element.64), channel_id=1, source_target_pairs={{0,16},{4,20},{8,24},{12,28},{16,0},{20,4},{24,8},{28,12},{1,17},{... | collective-permute-start | bytes 55304 | tf_op jit(solution)/shard_map/ppermute | solution.py:354
  29.2 7.1 %slice-start.7 = ((s8[5505024]{0:T(1024)(128)(4,1)}), s8[4194304]{0:T(1024)(128)(4,1)S(1)}, s32[]{:S(2)}) async-start(s8[5505024]{0:T(1024)(128)(4,1)} %bitcast.19), calls=%async_computation.7 | async-start | bytes 8388608
  29.2 7.1 %slice-start.9 = ((s8[5505024]{0:T(1024)(128)(4,1)}), s8[4194304]{0:T(1024)(128)(4,1)S(1)}, s32[]{:S(2)}) async-start(s8[5505024]{0:T(1024)(128)(4,1)} %bitcast.21), calls=%async_computation.9 | async-start | bytes 8388608
  29.2 7.1 %slice-start.8 = ((s8[5505024]{0:T(1024)(128)(4,1)}), s8[1310720]{0:T(1024)(128)(4,1)S(1)}, s32[]{:S(2)}) async-start(s8[5505024]{0:T(1024)(128)(4,1)} %bitcast.19), calls=%async_computation.8 | async-start | bytes 2621440
  29.2 7.1 %slice-start.10 = ((s8[5505024]{0:T(1024)(128)(4,1)}), s8[1310720]{0:T(1024)(128)(4,1)S(1)}, s32[]{:S(2)}) async-start(s8[5505024]{0:T(1024)(128)(4,1)} %bitcast.21), calls=%async_computation.10 | async-start | bytes 2621440
  29.2 8.8 %collective-permute-start.6 = (bf16[9,8,128]{2,1,0:T(8,128)(2,1)S(1)}, bf16[9,8,128]{2,1,0:T(8,128)(2,1)S(1)}, u32[]{:S(2)}, u32[]{:S(2)}) collective-permute-start(bf16[9,8,128]{2,1,0:T(8,128)(2,1)S(1)} %get-tuple-element.63), channel_id=1, source_target_pairs={{0,24},{4,28},{8,16},{12,20},{16,8},{20,12},{24,0},{28,4},{1,25},{... | collective-permute-start | bytes 55304 | tf_op jit(solution)/shard_map/ppermute | solution.py:354
  31.0 7.0 %slice-start = ((s8[11010048]{0:T(1024)(128)(4,1)}), s8[4194304]{0:T(1024)(128)(4,1)S(1)}, s32[]{:S(2)}) async-start(s8[11010048]{0:T(1024)(128)(4,1)} %bitcast.13), calls=%async_computation | async-start | bytes 8388608
  31.0 7.5 %slice-start.1 = ((s8[11010048]{0:T(1024)(128)(4,1)}), s8[4194304]{0:T(1024)(128)(4,1)S(1)}, s32[]{:S(2)}) async-start(s8[11010048]{0:T(1024)(128)(4,1)} %bitcast.13), calls=%async_computation.1 | async-start | bytes 8388608
  36.3 2.9 %slice-start.2 = ((s8[11010048]{0:T(1024)(128)(4,1)}), s8[2621440]{0:T(1024)(128)(4,1)S(1)}, s32[]{:S(2)}) async-start(s8[11010048]{0:T(1024)(128)(4,1)} %bitcast.13), calls=%async_computation.2 | async-start | bytes 5242880
  37.9 6.5 %copy-start.1 = (f32[1344]{0:T(1024)S(1)}, f32[1344]{0:T(1024)}, u32[]{:S(2)}) copy-start(f32[1344]{0:T(1024)} %param.25) | copy-start | bytes 16132
  37.9 11.4 %copy-start = (bf16[8,5376]{1,0:T(8,128)(2,1)S(1)}, bf16[8,5376]{1,0:T(8,128)(2,1)}, u32[]{:S(2)}) copy-start(bf16[8,5376]{1,0:T(8,128)(2,1)} %refs_4_.5) | copy-start | bytes 258052
  40.9 4.5 %collective-permute-start.7 = (bf16[8,5376]{1,0:T(8,128)(2,1)S(1)}, bf16[8,5376]{1,0:T(8,128)(2,1)S(1)}, u32[]{:S(2)}, u32[]{:S(2)}) collective-permute-start(bf16[8,5376]{1,0:T(8,128)(2,1)S(1)} %get-tuple-element.61), channel_id=1, source_target_pairs={{0,1},{1,0},{2,3},{3,2},{4,5},{5,4},{6,7},{7,6},{8,9},{9,8},{10,11... | collective-permute-start | bytes 258056 | tf_op jit(solution)/shard_map/ppermute | solution.py:354
  42.4 5.4 %collective-permute-start.8 = (bf16[8,5376]{1,0:T(8,128)(2,1)S(1)}, bf16[8,5376]{1,0:T(8,128)(2,1)S(1)}, u32[]{:S(2)}, u32[]{:S(2)}) collective-permute-start(bf16[8,5376]{1,0:T(8,128)(2,1)S(1)} %get-tuple-element.61), channel_id=1, source_target_pairs={{0,2},{1,3},{2,0},{3,1},{4,6},{5,7},{6,4},{7,5},{8,10},{9,11},{10,... | collective-permute-start | bytes 258056 | tf_op jit(solution)/shard_map/ppermute | solution.py:354
  43.9 5.4 %collective-permute-start.9 = (bf16[8,5376]{1,0:T(8,128)(2,1)S(1)}, bf16[8,5376]{1,0:T(8,128)(2,1)S(1)}, u32[]{:S(2)}, u32[]{:S(2)}) collective-permute-start(bf16[8,5376]{1,0:T(8,128)(2,1)S(1)} %get-tuple-element.61), channel_id=1, source_target_pairs={{0,3},{1,2},{2,1},{3,0},{4,7},{5,6},{6,5},{7,4},{8,11},{9,10},{10,... | collective-permute-start | bytes 258056 | tf_op jit(solution)/shard_map/ppermute | solution.py:354
where the time goes:
time: 50.3 us; the launch traced here: 50.1 us
  Pallas kernels  22.4 us (45%)
  starting transfers between devices  16.5 us (33%)
  waiting for transfers between devices  9.55 us (19%)
  local copies, waits for them, and re-layouts  1.29 us (3%)
    ppermute x10, starting transfers between devices, swap(): return lax.ppermute(x, axis, [(i, i ^ k) for i in range(n)])  16.5 us
    pallas_call x2, Pallas kernels, body(): pl.pallas_call(functools.partial(text_kernel, first, slots if lead else 0...  10.5 us
    ppermute x10, waiting for transfers between devices, swap(): return lax.ppermute(x, axis, [(i, i ^ k) for i in range(n)])  9.55 us
    pallas_call x1, Pallas kernels, body(): pl.pallas_call(functools.partial(query_kernel, scale, size), out_shape=(j...  5.49 us
    pallas_call x1, Pallas kernels, body(): pl.pallas_call(functools.partial(image_kernel, batch, len(queries)), out_...  2.36 us
    pallas_call x1, Pallas kernels, body(): pl.pallas_call(functools.partial(out_kernel, o_size, len(images), len(tex...  1.71 us
    pallas_call x1, Pallas kernels, body(): pl.pallas_call(kv_kernel, out_shape=(jax.ShapeDtypeStruct((rows, heads, d...  1.56 us
    unnamed x26, local copies, waits for them, and re-layouts  1.29 us
  transfers between devices with their start and end apart: 10, of which 6 were waited for; matrix products, arithmetic and copies ran while one was open for 0% of the time, Pallas kernels for 24%

commit v1 on v0

--- a/solution.py
+++ b/solution.py
@@ -11,7 +11,9 @@
 
 EPS = 1e-06
 NEG = -1e30
+BLOCK = 128
 SMALL = 4 << 20
+SIZES = 64
 F32 = jnp.float32
 BF16 = jnp.bfloat16
 HBM = pl.BlockSpec(memory_space=pltpu.HBM)
@@ -46,14 +48,15 @@
 
 
 def query_kernel(
-    scale, size, freq, hidden, gain, q_gain_in, k_gain, position_in, owner, count, slot, weight,
-    q_out, normed_out, cos_out, sin_out, k_gain_out, position, owner_out, count_out, slot_out,
-    w_buf, h_buf, g_buf, q_gain, heads_buf, w_sem, s_sem
+    scale, size, slots, freq, hidden, gain, q_gain_in, k_gain, position_in, owner, count, slot, weight,
+    q_out, normed_out, cos_out, sin_out, k_gain_out, codes,
+    w_buf, h_buf, g_buf, q_gain, heads_buf, position, owner_buf, count_buf, slot_buf, w_sem, s_sem
 ):
     copies = row_copies(weight, w_buf, w_sem, size)
     pairs = (
         (hidden, h_buf), (gain, g_buf), (position_in, position), (q_gain_in, q_gain),
-        (k_gain, k_gain_out), (owner, owner_out), (count, count_out), (slot, slot_out),
+        (k_gain, k_gain_out),
+        (owner, owner_buf), (count, count_buf), (slot, slot_buf),
     )
     small = [pltpu.make_async_copy(a, b, s_sem.at[i]) for i, (a, b) in enumerate(pairs)]
     for c in small[:2] + copies[:1] + small[2:] + copies[1:]:
@@ -91,6 +94,9 @@
             sin_out[...] = sine
     for c in small[3:]:
         c.wait()
+    request = lax.broadcasted_iota(jnp.int32, codes.shape, 1)
+    code = (request * slots + slot_buf[...]) * SIZES + count_buf[...] // BLOCK
+    codes[...] = jnp.where(owner_buf[...] == lax.axis_index("grp"), code, -1)
     cosine, sine = cos_out[...], sin_out[...]
     for n in range(acc.shape[1] // dim):
         v = rms_rope(acc[:, n * dim : (n + 1) * dim], q_gain[...], cosine, sine)
@@ -154,26 +160,20 @@
     return top, total, gather_heads(summed, heads, dim)
 
 
-def plan(slots, owner, count, slot, item, length, filled):
-    me = lax.axis_index("grp")
-
+def plan_kernel(slots, codes, item):
     def note(r, have):
-        hit = owner[r] == me
-        at = jnp.where(hit, have, slots)
-        item[at] = r * slots + slot[r]
-        length[at] = count[r]
+        code = codes[0, r]
+        hit = code >= 0
+        item[jnp.where(hit, have, slots)] = code
         return have + hit.astype(jnp.int32)
 
-    filled[0] = lax.fori_loop(0, owner.shape[0], note, jnp.int32(0), unroll=8)
-
-
-def text_kernel(first, slots, position, q, *refs):
-    if slots:
-        owner, count_in, slot_in = refs[:3]
-        keys, values, o_out, m_out, l_out, item, length, filled = refs[3:11]
-        k_buf, v_buf, k_sem, v_sem = refs[11:]
-    else:
-        keys, values, o_out, m_out, l_out, k_buf, v_buf, k_sem, v_sem = refs
+    item[slots + 1] = lax.fori_loop(0, codes.shape[1], note, jnp.int32(0), unroll=16)
+
+
+def text_kernel(
+    first, q, position_in, keys, values, o_out, m_out, l_out, k_buf, v_buf, position, k_sem, v_sem,
+    p_sem
+):
     count, window, _ = k_buf.shape
     heads, dim = q.shape[1:]
     copies = [
@@ -183,11 +183,14 @@
         ]
         for i in range(count)
     ]
-    for pair in copies:
+    table = pltpu.make_async_copy(position_in, position, p_sem)
+    copies[0][0].start()
+    table.start()
+    copies[0][1].start()
+    for pair in copies[1:]:
         for c in pair:
             c.start()
-    if slots:
-        plan(slots, owner, count_in, slot_in, item, length, filled)
+    table.wait()
     column = lax.broadcasted_iota(jnp.int32, (heads, window), 1)
 
     def score(i):
@@ -209,7 +212,7 @@
         scores = later
 
 
-def image_kernel(batch, n_q, item, tokens, filled, *refs):
+def image_kernel(batch, n_q, item, *refs):
     queries = refs[:n_q]
     keys, values, mine, other, q_buf, s_buf, out_buf = refs[n_q:]
     me = lax.axis_index("grp")
@@ -217,7 +220,7 @@
     rows = queries[0].shape[0]
     heads, dim = queries[0].shape[1:]
     half = mine.shape[0]
-    have = filled[0]
+    have = item[slots + 1]
     out_buf[...] = jnp.zeros_like(out_buf)
     known, step = [0], half
     q_buf[:rows] = queries[0][...]
@@ -236,20 +239,22 @@
             n = t * batch + u
             live = n < have
             n = jnp.minimum(n, have - 1)
-            r = item[n] // slots
-            found.append((n, live, r, item[n] - r * slots))
+            code = item[n]
+            both = code // SIZES
+            r = both // slots
+            found.append((live, r, both - r * slots, (code - both * SIZES) * BLOCK))
         return found
 
     def score(t):
-        for u, (n, live, r, place) in enumerate(members(t)):
+        for u, (live, r, place, tokens) in enumerate(members(t)):
             group, lane = lax.bitwise_xor(r // rows, me), lax.rem(r, rows)
             s_buf[lax.rem(t, 2), u] = score_block(
-                q_buf[group * rows + lane], keys[place], column < tokens[n]
+                q_buf[group * rows + lane], keys[place], column < tokens
             )
 
     def weigh(t):
         done = []
-        for u, (n, live, r, place) in enumerate(members(t)):
+        for u, (live, r, place, tokens) in enumerate(members(t)):
             top, total, summed = weigh_block(s_buf[lax.rem(t, 2), u], values[place], heads, dim)
             mean = (summed / total).astype(BF16)
             group, lane = lax.bitwise_xor(r // rows, me), lax.rem(r, rows)
@@ -372,26 +377,29 @@
 
     size = pieces_of(width, 768)
     n_copies = width // size
-    whole = jax.ShapeDtypeStruct(image_owner.shape, jnp.int32)
-    q, normed, cosine, sine, k_gain, position, owner, count, slot = pl.pallas_call(
-        functools.partial(query_kernel, scale, size),
+    every = (1, groups * rows)
+    q, normed, cosine, sine, k_gain, codes = pl.pallas_call(
+        functools.partial(query_kernel, scale, size, slots),
         out_shape=(
             jax.ShapeDtypeStruct((rows, heads, dim), BF16),
             jax.ShapeDtypeStruct((rows, width), BF16),
             jax.ShapeDtypeStruct((rows, dim), F32),
             jax.ShapeDtypeStruct((rows, dim), F32),
             jax.ShapeDtypeStruct((1, dim), F32),
-            jax.ShapeDtypeStruct((rows,), jnp.int32),
-            whole, whole, whole,
+            jax.ShapeDtypeStruct(every, jnp.int32),
         ),
         in_specs=[VMEM] + [HBM] * 9,
-        out_specs=(VMEM,) * 5 + (SMEM,) * 4,
+        out_specs=(VMEM,) * 6,
         scratch_shapes=[
             pltpu.VMEM(query_weight.shape, BF16),
             pltpu.VMEM(hidden.shape, BF16),
             pltpu.VMEM((width // dim, dim), F32),
             pltpu.VMEM((1, dim), F32),
             pltpu.VMEM((rows, heads, dim), F32),
+            pltpu.SMEM(text_position.shape, jnp.int32),
+            pltpu.VMEM(every, jnp.int32),
+            pltpu.VMEM(every, jnp.int32),
+            pltpu.VMEM(every, jnp.int32),
             pltpu.SemaphoreType.DMA((n_copies,)),
             pltpu.SemaphoreType.DMA((8,)),
         ],
@@ -404,8 +412,8 @@
             stay,
             (
                 hidden, pre_gain.reshape(-1, dim), query_norm_gain.reshape(1, -1),
-                key_gain.reshape(1, -1), text_position, image_owner, image_count, image_slot,
-                query_weight,
+                key_gain.reshape(1, -1), text_position, image_owner.reshape(1, -1),
+                image_count.reshape(1, -1), image_slot.reshape(1, -1), query_weight,
             ),
         ),
     )
@@ -421,38 +429,41 @@
             held = jnp.concatenate([held, got], axis=0)
 
     text = []
-    for n, (first, last) in enumerate(text_parts(rows)):
+    for first, last in text_parts(rows):
         part = (last - first,) + text_keys.shape[1:]
         share = math.prod(part)
-        lead = n == 0
-        got = pl.pallas_call(
-            functools.partial(text_kernel, first, slots if lead else 0),
-            out_shape=(jax.ShapeDtypeStruct((last - first, heads, dim), F32),) * 3
-            + lead * (
-                jax.ShapeDtypeStruct((slots + 1,), jnp.int32),
-                jax.ShapeDtypeStruct((slots + 1,), jnp.int32),
-                jax.ShapeDtypeStruct((1,), jnp.int32),
-            ),
-            in_specs=[SMEM, VMEM] + lead * [SMEM] * 3 + [HBM, HBM],
-            out_specs=(VMEM,) * 3 + lead * (SMEM,) * 3,
+        text += pl.pallas_call(
+            functools.partial(text_kernel, first),
+            out_shape=(jax.ShapeDtypeStruct((last - first, heads, dim), F32),) * 3,
+            in_specs=[VMEM, HBM, HBM, HBM],
+            out_specs=(VMEM,) * 3,
             scratch_shapes=[
                 pltpu.VMEM(part, BF16),
                 pltpu.VMEM(part, BF16),
+                pltpu.SMEM(text_position.shape, jnp.int32),
                 pltpu.SemaphoreType.DMA(part[:1]),
                 pltpu.SemaphoreType.DMA(part[:1]),
+                pltpu.SemaphoreType.DMA,
             ],
             compiler_params=pltpu.CompilerParams(vmem_limit_bytes=4 * share + SMALL),
             cost_estimate=cost(8 * heads * share, 4 * share),
-        )(position, q, *(lead * (owner, count, slot)), stay(text_keys), stay(text_values))
-        text += got[:3]
-        if lead:
-            items = got[3:]
+        )(q, *map(stay, (text_position, text_keys, text_values)))
+
+    item = pl.pallas_call(
+        functools.partial(plan_kernel, slots),
+        out_shape=jax.ShapeDtypeStruct((slots + 2,), jnp.int32),
+        in_specs=[SMEM],
+        out_specs=SMEM,
+        compiler_params=pltpu.CompilerParams(vmem_limit_bytes=SMALL),
+        cost_estimate=cost(1 << 20, 1 << 20),
+        name="plan",
+    )(codes)
 
     batch = 8
     mine, other = pl.pallas_call(
         functools.partial(image_kernel, batch, len(queries)),
         out_shape=(jax.ShapeDtypeStruct((groups // 2, rows + 1, heads, dim), BF16),) * 2,
-        in_specs=[SMEM] * 3 + [VMEM] * (len(queries) + 2),
+        in_specs=[SMEM] + [VMEM] * (len(queries) + 2),
         out_specs=(VMEM, VMEM),
         scratch_shapes=[
             pltpu.VMEM((groups * rows, heads, dim), BF16),
@@ -462,7 +473,7 @@
         compiler_params=pltpu.CompilerParams(vmem_limit_bytes=SMALL),
         cost_estimate=cost(8 * heads * image_keys.size, 4 * image_keys.size),
         name="image",
-    )(*items, *queries, image_keys, image_values)
+    )(item, *queries, image_keys, image_values)
 
     key_weight, value_weight, out_weight, mine, other = lax.optimization_barrier(
         (key_weight, value_weight, out_weight, mine, other)

time: 50.3 us -> 51.2 us (1.018)
  local copies, waits for them, and re-layouts: 1.29 us -> 4.52 us
  Pallas kernels: 22.4 us -> 20.9 us
  waiting for transfers between devices: 9.55 us -> 8.7 us
    unnamed x26 -> x24, local copies, waits for them, and re-layouts: 1.29 us -> 4.51 us
    ppermute x10, waiting for transfers between devices: 9.55 us -> 8.7 us  [swap(): return lax.ppermute(x, axis, [(i, i ^ k) for i in range(n)])]
    pallas_call x3 -> x4, Pallas kernels: 16 us -> 15.2 us  [the longest x2 8.78 us: body(): pl.pallas_call(functools.partial(text_kernel, first), out_shape=(jax.Shap...]
    pallas_call x1, Pallas kernels: 2.36 us -> 1.72 us  [body(): pl.pallas_call(functools.partial(image_kernel, batch, len(queries)), out_...]
  transfers between devices with their start and end apart: 10 -> 10, of which waited for: 6 -> 5; matrix products, arithmetic and copies ran while one was open for 0% -> 0% of each run, Pallas kernels for 24% -> 23%
where the time goes in v1:
time: 51.2 us; the launch traced here: 51.1 us
  Pallas kernels  20.9 us (41%)
  starting transfers between devices  16.6 us (32%)
  waiting for transfers between devices  8.7 us (17%)
  local copies, waits for them, and re-layouts  4.52 us (9%)
    ppermute x10, starting transfers between devices, swap(): return lax.ppermute(x, axis, [(i, i ^ k) for i in range(n)])  16.6 us
    pallas_call x2, Pallas kernels, body(): pl.pallas_call(functools.partial(text_kernel, first), out_shape=(jax.Shap...  8.78 us
    ppermute x10, waiting for transfers between devices, swap(): return lax.ppermute(x, axis, [(i, i ^ k) for i in range(n)])  8.7 us
    pallas_call x1, Pallas kernels, body(): pl.pallas_call(functools.partial(query_kernel, scale, size, slots), out_s...  5.06 us
    unnamed x24, local copies, waits for them, and re-layouts  4.51 us
    pallas_call x1, Pallas kernels, body(): pl.pallas_call(functools.partial(image_kernel, batch, len(queries)), out_...  1.72 us
    pallas_call x1, Pallas kernels, body(): pl.pallas_call(functools.partial(out_kernel, o_size, len(images), len(tex...  1.71 us
    pallas_call x1, Pallas kernels, body(): pl.pallas_call(kv_kernel, out_shape=(jax.ShapeDtypeStruct((rows, heads, d...  1.56 us
  transfers between devices with their start and end apart: 10, of which 5 were waited for; matrix products, arithmetic and copies ran while one was open for 0% of the time, Pallas kernels for 23%

profile of v1, /device:TPU:0, one launch (start us, length us, event | category | flops | bytes accessed | tf_op | source)
XLA Modules:
  0.0 51.1 jit_solution(7562966225406100111)
XLA Ops:
  0.0 0.0 slice-start.3
  0.0 0.1 maximum_bitcast_fusion.freq
  0.1 0.0 slice-start.4
  0.1 5.1 %query.1 = (bf16[8,8,128]{2,1,0:T(8,128)(2,1)S(1)}, bf16[8,5376]{1,0:T(8,128)(2,1)S(1)}, f32[8,128]{1,0:T(8,128)S(1)}, f32[8,128]{1,0:T(8,128)S(1)}, f32[1,128]{1,0:T(1,128)S(1)}, /*index=5*/s32[1,64]{1,0:T(1,128)S(1)}) custom-call(f32[1,128]{1,0:T(1,128)S(1)} %maximum_bitcast_fusion.freq, bf16[8,5376]{1,0:T(8,128)(2,1)} %refs_4_.3, f32[42,128]{1,0:T(8,128)} %bitcast.24, ...), custom_call_target="tpu_custom_call" | custom-call | flops 88080384 | bytes 11010048 | tf_op jit(solution)/shard_map/query/pallas_call | solution.py:381
  5.2 4.1 %collective-permute-start = (bf16[8,8,128]{2,1,0:T(8,128)(2,1)S(1)}, bf16[8,8,128]{2,1,0:T(8,128)(2,1)S(1)}, u32[]{:S(2)}, u32[]{:S(2)}) collective-permute-start(bf16[8,8,128]{2,1,0:T(8,128)(2,1)S(1)} %get-tuple-element.29.refs_0_.q), channel_id=1, source_target_pairs={{0,16},{4,20},{8,24},{12,28},{16,0},{20,4},{24,8},{28,12},{1,17},{... | collective-permute-start | bytes 49160 | tf_op jit(solution)/shard_map/ppermute | solution.py:359
  9.3 1.7 %collective-permute-done.refs_1_ = bf16[8,8,128]{2,1,0:T(8,128)(2,1)S(1)} collective-permute-done((bf16[8,8,128]{2,1,0:T(8,128)(2,1)S(1)}, bf16[8,8,128]{2,1,0:T(8,128)(2,1)S(1)}, u32[]{:S(2)}, u32[]{:S(2)}) %collective-permute-start) | collective-permute-done | bytes 16416 | tf_op jit(solution)/shard_map/ppermute | solution.py:359
  11.0 1.9 %collective-permute-start.1 = (bf16[16,8,128]{2,1,0:T(8,128)(2,1)S(1)}, bf16[16,8,128]{2,1,0:T(8,128)(2,1)S(1)}, u32[]{:S(2)}, u32[]{:S(2)}) collective-permute-start(bf16[16,8,128]{2,1,0:T(8,128)(2,1)S(1)} %pad_maximum_fusion.1), channel_id=1, source_target_pairs={{0,8},{4,12},{8,0},{12,4},{16,24},{20,28},{24,16},{28,20},{1,9},{5... | collective-permute-start | bytes 98312 | tf_op jit(solution)/shard_map/ppermute | solution.py:359
  12.9 2.0 %collective-permute-done.1.refs_2_ = bf16[16,8,128]{2,1,0:T(8,128)(2,1)S(1)} collective-permute-done((bf16[16,8,128]{2,1,0:T(8,128)(2,1)S(1)}, bf16[16,8,128]{2,1,0:T(8,128)(2,1)S(1)}, u32[]{:S(2)}, u32[]{:S(2)}) %collective-permute-start.1) | collective-permute-done | bytes 32800 | tf_op jit(solution)/shard_map/ppermute | solution.py:359
  14.9 0.1 collective-permute-start.2
  15.0 1.3 %plan.1.item = s32[26]{0:T(128)S(1)} custom-call(s32[1,64]{1,0:T(1,128)S(1)} %get-tuple-element.28.codes), custom_call_target="tpu_custom_call" | custom-call | flops 1048576 | bytes 1048576 | tf_op jit(solution)/shard_map/plan/pallas_call | solution.py:452
  16.3 0.0 collective-permute-done.2.refs_3_
  16.4 0.0 slice-done.3
  16.4 0.0 slice-done.4
  16.4 0.0 copy-start
  16.4 2.8 %copy-done = bf16[24,256,512]{2,1,0:T(8,128)(2,1)S(1)} copy-done((bf16[24,256,512]{2,1,0:T(8,128)(2,1)S(1)}, bf16[24,256,512]{2,1,0:T(8,128)(2,1)}, u32[]{:S(2)}) %copy-start) | copy-done | bytes 6291480
  19.2 1.7 %image.1 = (bf16[4,9,8,128]{3,2,1,0:T(8,128)(2,1)S(1)}, bf16[4,9,8,128]{3,2,1,0:T(8,128)(2,1)S(1)}) custom-call(s32[26]{0:T(128)S(1)} %plan.1.item, bf16[8,8,128]{2,1,0:T(8,128)(2,1)S(1)} %get-tuple-element.29.refs_0_.q, bf16[8,8,128]{2,1,0:T(8,128)(2,1)S(1)} %collective-permute-done.refs_1_, bf16[16,8,128]{2,1,0:T(8,128)(2,1)S(1)} %collective-permute-done.1.refs_2_, ...), custom_call_target="tpu_custom_call" | custom-call | flops 201326592 | bytes 12582912 | tf_op jit(solution)/shard_map/image/pallas_call | solution.py:463
  20.9 2.5 %collective-permute-start.3 = (bf16[4,9,8,128]{3,2,1,0:T(8,128)(2,1)S(1)}, bf16[4,9,8,128]{3,2,1,0:T(8,128)(2,1)S(1)}, u32[]{:S(2)}, u32[]{:S(2)}) collective-permute-start(bf16[4,9,8,128]{3,2,1,0:T(8,128)(2,1)S(1)} %get-tuple-element.33), channel_id=1, source_target_pairs={{0,4},{4,0},{8,12},{12,8},{16,20},{20,16},{24,28},{28,24},{1,5},{5... | collective-permute-start | bytes 221192 | tf_op jit(solution)/shard_map/ppermute | solution.py:359
  23.4 4.0 %shard_map.163 = (f32[4,8,128]{2,1,0:T(8,128)S(1)}, f32[4,8,128]{2,1,0:T(8,128)S(1)}, f32[4,8,128]{2,1,0:T(8,128)S(1)}) custom-call(bf16[8,8,128]{2,1,0:T(8,128)(2,1)S(1)} %get-tuple-element.29.refs_0_.q, s32[8]{0:T(128)} %position_in.5, bf16[8,1024,512]{2,1,0:T(8,128)(2,1)} %keys.3, bf16[8,1024,512]{2,1,0:T(8,128)(2,1)} %values.3), custom_call_target="tpu_custom_call" | custom-call | flops 134217728 | bytes 8388608 | tf_op jit(solution)/shard_map/pallas_call | solution.py:435
  27.4 0.0 collective-permute-done.3
  27.4 0.1 collective-permute-start.4
  27.5 2.6 %collective-permute-start.5 = (bf16[9,8,128]{2,1,0:T(8,128)(2,1)S(1)}, bf16[9,8,128]{2,1,0:T(8,128)(2,1)S(1)}, u32[]{:S(2)}, u32[]{:S(2)}) collective-permute-start(bf16[9,8,128]{2,1,0:T(8,128)(2,1)S(1)} %get-tuple-element.52), channel_id=1, source_target_pairs={{0,16},{4,20},{8,24},{12,28},{16,0},{20,4},{24,8},{28,12},{1,17},{... | collective-permute-start | bytes 55304 | tf_op jit(solution)/shard_map/ppermute | solution.py:359
  30.1 0.0 slice-start.5
  30.1 0.0 slice-start.7
  30.1 0.0 slice-start.6
  30.1 0.0 slice-start.8
  30.2 1.8 %collective-permute-start.6 = (bf16[9,8,128]{2,1,0:T(8,128)(2,1)S(1)}, bf16[9,8,128]{2,1,0:T(8,128)(2,1)S(1)}, u32[]{:S(2)}, u32[]{:S(2)}) collective-permute-start(bf16[9,8,128]{2,1,0:T(8,128)(2,1)S(1)} %get-tuple-element.51), channel_id=1, source_target_pairs={{0,24},{4,28},{8,16},{12,20},{16,8},{20,12},{24,0},{28,4},{1,25},{... | collective-permute-start | bytes 55304 | tf_op jit(solution)/shard_map/ppermute | solution.py:359
  31.9 0.0 slice-start
  31.9 0.0 slice-start.1
  31.9 4.8 %shard_map.164 = (f32[4,8,128]{2,1,0:T(8,128)S(1)}, f32[4,8,128]{2,1,0:T(8,128)S(1)}, f32[4,8,128]{2,1,0:T(8,128)S(1)}) custom-call(bf16[8,8,128]{2,1,0:T(8,128)(2,1)S(1)} %get-tuple-element.29.refs_0_.q, s32[8]{0:T(128)} %position_in.5, bf16[8,1024,512]{2,1,0:T(8,128)(2,1)} %keys.3, bf16[8,1024,512]{2,1,0:T(8,128)(2,1)} %values.3), custom_call_target="tpu_custom_call" | custom-call | flops 134217728 | bytes 8388608 | tf_op jit(solution)/shard_map/pallas_call | solution.py:435
  36.7 0.0 slice-done.5
  36.7 0.0 slice-done.7
  36.7 0.0 slice-done.6
  36.8 0.0 slice-done.8
  36.8 0.0 slice-start.2
  36.8 1.6 %keyvalue.1 = (f32[8,8,128]{2,1,0:T(8,128)S(1)}, f32[8,8,128]{2,1,0:T(8,128)S(1)}) custom-call(bf16[8,5376]{1,0:T(8,128)(2,1)S(1)} %get-tuple-element.40.normed, f32[8,128]{1,0:T(8,128)S(1)} %get-tuple-element.41.cosine, f32[8,128]{1,0:T(8,128)S(1)} %get-tuple-element.42.sine, f32[1,128]{1,0:T(1,128)S(1)} %get-tuple-element.43.k_gain, ...), custom_call_target="tpu_custom_call" | custom-call | flops 88080384 | bytes 11010048 | tf_op jit(solution)/shard_map/keyvalue/pallas_call | solution.py:481
  38.4 0.0 copy-start.2
  38.4 0.0 copy-start.1
  38.4 0.0 collective-permute-done.4.refs_1_
  38.4 0.0 collective-permute-done.5.refs_2_
  38.4 0.0 collective-permute-done.6.refs_3_
  38.4 0.0 slice-done
  38.4 1.0 %slice-done.1 = s8[4194304]{0:T(1024)(128)(4,1)S(1)} async-done(((s8[11010048]{0:T(1024)(128)(4,1)}), s8[4194304]{0:T(1024)(128)(4,1)S(1)}, s32[]{:S(2)}) %slice-start.1) | async-done | bytes 4194328
  39.4 0.7 %slice-done.2 = s8[2621440]{0:T(1024)(128)(4,1)S(1)} async-done(((s8[11010048]{0:T(1024)(128)(4,1)}), s8[2621440]{0:T(1024)(128)(4,1)S(1)}, s32[]{:S(2)}) %slice-start.2) | async-done | bytes 2621464
  40.1 1.7 %project.1 = (bf16[8,5376]{1,0:T(8,128)(2,1)S(1)}, f32[8,5376]{1,0:T(8,128)S(1)}) custom-call(bf16[9,8,128]{2,1,0:T(8,128)(2,1)S(1)} %get-tuple-element.54.refs_0_, bf16[9,8,128]{2,1,0:T(8,128)(2,1)S(1)} %collective-permute-done.4.refs_1_, bf16[9,8,128]{2,1,0:T(8,128)(2,1)S(1)} %collective-permute-done.5.refs_2_, ...), custom_call_target="tpu_custom_call" | custom-call | flops 88080384 | bytes 11010048 | tf_op jit(solution)/shard_map/project/pallas_call | solution.py:499
  41.8 1.6 %collective-permute-start.7 = (bf16[8,5376]{1,0:T(8,128)(2,1)S(1)}, bf16[8,5376]{1,0:T(8,128)(2,1)S(1)}, u32[]{:S(2)}, u32[]{:S(2)}) collective-permute-start(bf16[8,5376]{1,0:T(8,128)(2,1)S(1)} %get-tuple-element.49), channel_id=1, source_target_pairs={{0,1},{1,0},{2,3},{3,2},{4,5},{5,4},{6,7},{7,6},{8,9},{9,8},{10,11... | collective-permute-start | bytes 258056 | tf_op jit(solution)/shard_map/ppermute | solution.py:359
  43.4 1.5 %collective-permute-start.8 = (bf16[8,5376]{1,0:T(8,128)(2,1)S(1)}, bf16[8,5376]{1,0:T(8,128)(2,1)S(1)}, u32[]{:S(2)}, u32[]{:S(2)}) collective-permute-start(bf16[8,5376]{1,0:T(8,128)(2,1)S(1)} %get-tuple-element.49), channel_id=1, source_target_pairs={{0,2},{1,3},{2,0},{3,1},{4,6},{5,7},{6,4},{7,5},{8,10},{9,11},{10,... | collective-permute-start | bytes 258056 | tf_op jit(solution)/shard_map/ppermute | solution.py:359
  44.9 0.4 collective-permute-start.9
  45.3 0.0 copy-done.2
  45.3 1.0 %collective-permute-done.7.refs_0_ = bf16[8,5376]{1,0:T(8,128)(2,1)S(1)} collective-permute-done((bf16[8,5376]{1,0:T(8,128)(2,1)S(1)}, bf16[8,5376]{1,0:T(8,128)(2,1)S(1)}, u32[]{:S(2)}, u32[]{:S(2)}) %collective-permute-start.7) | collective-permute-done | bytes 86048 | tf_op jit(solution)/shard_map/ppermute | solution.py:359
  46.3 2.5 %collective-permute-done.8.refs_1_ = bf16[8,5376]{1,0:T(8,128)(2,1)S(1)} collective-permute-done((bf16[8,5376]{1,0:T(8,128)(2,1)S(1)}, bf16[8,5376]{1,0:T(8,128)(2,1)S(1)}, u32[]{:S(2)}, u32[]{:S(2)}) %collective-permute-start.8) | collective-permute-done | bytes 86048 | tf_op jit(solution)/shard_map/ppermute | solution.py:359
  48.8 1.5 %collective-permute-done.9.refs_2_ = bf16[8,5376]{1,0:T(8,128)(2,1)S(1)} collective-permute-done((bf16[8,5376]{1,0:T(8,128)(2,1)S(1)}, bf16[8,5376]{1,0:T(8,128)(2,1)S(1)}, u32[]{:S(2)}, u32[]{:S(2)}) %collective-permute-start.9) | collective-permute-done | bytes 86048 | tf_op jit(solution)/shard_map/ppermute | solution.py:359
  50.3 0.0 copy-done.1
  50.3 0.8 %finish.1 = bf16[8,1344]{1,0:T(8,128)(2,1)} custom-call(bf16[8,5376]{1,0:T(8,128)(2,1)S(1)} %collective-permute-done.7.refs_0_, bf16[8,5376]{1,0:T(8,128)(2,1)S(1)} %collective-permute-done.8.refs_1_, bf16[8,5376]{1,0:T(8,128)(2,1)S(1)} %collective-permute-done.9.refs_2_, f32[8,5376]{1,0:T(8,128)S(1)} %get-tuple-element.50.refs_3_, ...), custom_call_target="tpu_custom_call" | custom-call | flops 344064 | bytes 688128 | tf_op jit(solution)/shard_map/finish/pallas_call | solution.py:514
  (9 shorter events, 0.1 us)
Async XLA Ops:
  0.0 16.4 %slice-start.3 = ((s8[6291456]{0:T(1024)(128)(4,1)}), s8[4194304]{0:T(1024)(128)(4,1)S(1)}, s32[]{:S(2)}) async-start(s8[6291456]{0:T(1024)(128)(4,1)} %bitcast.18), calls=%async_computation.3 | async-start | bytes 8388608
  0.1 16.3 %slice-start.4 = ((s8[6291456]{0:T(1024)(128)(4,1)}), s8[2097152]{0:T(1024)(128)(4,1)S(1)}, s32[]{:S(2)}) async-start(s8[6291456]{0:T(1024)(128)(4,1)} %bitcast.18), calls=%async_computation.4 | async-start | bytes 4194304
  5.2 5.8 %collective-permute-start = (bf16[8,8,128]{2,1,0:T(8,128)(2,1)S(1)}, bf16[8,8,128]{2,1,0:T(8,128)(2,1)S(1)}, u32[]{:S(2)}, u32[]{:S(2)}) collective-permute-start(bf16[8,8,128]{2,1,0:T(8,128)(2,1)S(1)} %get-tuple-element.29.refs_0_.q), channel_id=1, source_target_pairs={{0,16},{4,20},{8,24},{12,28},{16,0},{20,4},{24,8},{28,12},{1,17},{... | collective-permute-start | bytes 49160 | tf_op jit(solution)/shard_map/ppermute | solution.py:359
  11.0 3.9 %collective-permute-start.1 = (bf16[16,8,128]{2,1,0:T(8,128)(2,1)S(1)}, bf16[16,8,128]{2,1,0:T(8,128)(2,1)S(1)}, u32[]{:S(2)}, u32[]{:S(2)}) collective-permute-start(bf16[16,8,128]{2,1,0:T(8,128)(2,1)S(1)} %pad_maximum_fusion.1), channel_id=1, source_target_pairs={{0,8},{4,12},{8,0},{12,4},{16,24},{20,28},{24,16},{28,20},{1,9},{5... | collective-permute-start | bytes 98312 | tf_op jit(solution)/shard_map/ppermute | solution.py:359
  14.9 1.4 %collective-permute-start.2 = (bf16[32,8,128]{2,1,0:T(8,128)(2,1)S(1)}, bf16[32,8,128]{2,1,0:T(8,128)(2,1)S(1)}, u32[]{:S(2)}, u32[]{:S(2)}) collective-permute-start(bf16[32,8,128]{2,1,0:T(8,128)(2,1)S(1)} %pad_maximum_fusion), channel_id=1, source_target_pairs={{0,4},{4,0},{8,12},{12,8},{16,20},{20,16},{24,28},{28,24},{1,5},{5... | collective-permute-start | bytes 196616 | tf_op jit(solution)/shard_map/ppermute | solution.py:359
  16.4 2.8 %copy-start = (bf16[24,256,512]{2,1,0:T(8,128)(2,1)S(1)}, bf16[24,256,512]{2,1,0:T(8,128)(2,1)}, u32[]{:S(2)}) copy-start(bf16[24,256,512]{2,1,0:T(8,128)(2,1)} %refs_5_.1) | copy-start | bytes 18874372
  20.9 6.5 %collective-permute-start.3 = (bf16[4,9,8,128]{3,2,1,0:T(8,128)(2,1)S(1)}, bf16[4,9,8,128]{3,2,1,0:T(8,128)(2,1)S(1)}, u32[]{:S(2)}, u32[]{:S(2)}) collective-permute-start(bf16[4,9,8,128]{3,2,1,0:T(8,128)(2,1)S(1)} %get-tuple-element.33), channel_id=1, source_target_pairs={{0,4},{4,0},{8,12},{12,8},{16,20},{20,16},{24,28},{28,24},{1,5},{5... | collective-permute-start | bytes 221192 | tf_op jit(solution)/shard_map/ppermute | solution.py:359
  27.4 11.0 %collective-permute-start.4 = (bf16[9,8,128]{2,1,0:T(8,128)(2,1)S(1)}, bf16[9,8,128]{2,1,0:T(8,128)(2,1)S(1)}, u32[]{:S(2)}, u32[]{:S(2)}) collective-permute-start(bf16[9,8,128]{2,1,0:T(8,128)(2,1)S(1)} %get-tuple-element.53), channel_id=1, source_target_pairs={{0,8},{4,12},{8,0},{12,4},{16,24},{20,28},{24,16},{28,20},{1,9},{5... | collective-permute-start | bytes 55304 | tf_op jit(solution)/shard_map/ppermute | solution.py:359
  27.5 10.9 %collective-permute-start.5 = (bf16[9,8,128]{2,1,0:T(8,128)(2,1)S(1)}, bf16[9,8,128]{2,1,0:T(8,128)(2,1)S(1)}, u32[]{:S(2)}, u32[]{:S(2)}) collective-permute-start(bf16[9,8,128]{2,1,0:T(8,128)(2,1)S(1)} %get-tuple-element.52), channel_id=1, source_target_pairs={{0,16},{4,20},{8,24},{12,28},{16,0},{20,4},{24,8},{28,12},{1,17},{... | collective-permute-start | bytes 55304 | tf_op jit(solution)/shard_map/ppermute | solution.py:359
  30.1 6.6 %slice-start.5 = ((s8[5505024]{0:T(1024)(128)(4,1)}), s8[4194304]{0:T(1024)(128)(4,1)S(1)}, s32[]{:S(2)}) async-start(s8[5505024]{0:T(1024)(128)(4,1)} %bitcast.20), calls=%async_computation.5 | async-start | bytes 8388608
  30.1 6.6 %slice-start.7 = ((s8[5505024]{0:T(1024)(128)(4,1)}), s8[4194304]{0:T(1024)(128)(4,1)S(1)}, s32[]{:S(2)}) async-start(s8[5505024]{0:T(1024)(128)(4,1)} %bitcast.22), calls=%async_computation.7 | async-start | bytes 8388608
  30.1 6.6 %slice-start.6 = ((s8[5505024]{0:T(1024)(128)(4,1)}), s8[1310720]{0:T(1024)(128)(4,1)S(1)}, s32[]{:S(2)}) async-start(s8[5505024]{0:T(1024)(128)(4,1)} %bitcast.20), calls=%async_computation.6 | async-start | bytes 2621440
  30.1 6.6 %slice-start.8 = ((s8[5505024]{0:T(1024)(128)(4,1)}), s8[1310720]{0:T(1024)(128)(4,1)S(1)}, s32[]{:S(2)}) async-start(s8[5505024]{0:T(1024)(128)(4,1)} %bitcast.22), calls=%async_computation.8 | async-start | bytes 2621440
  30.2 8.3 %collective-permute-start.6 = (bf16[9,8,128]{2,1,0:T(8,128)(2,1)S(1)}, bf16[9,8,128]{2,1,0:T(8,128)(2,1)S(1)}, u32[]{:S(2)}, u32[]{:S(2)}) collective-permute-start(bf16[9,8,128]{2,1,0:T(8,128)(2,1)S(1)} %get-tuple-element.51), channel_id=1, source_target_pairs={{0,24},{4,28},{8,16},{12,20},{16,8},{20,12},{24,0},{28,4},{1,25},{... | collective-permute-start | bytes 55304 | tf_op jit(solution)/shard_map/ppermute | solution.py:359
  31.9 6.5 %slice-start = ((s8[11010048]{0:T(1024)(128)(4,1)}), s8[4194304]{0:T(1024)(128)(4,1)S(1)}, s32[]{:S(2)}) async-start(s8[11010048]{0:T(1024)(128)(4,1)} %bitcast.16), calls=%async_computation | async-start | bytes 8388608
  31.9 7.5 %slice-start.1 = ((s8[11010048]{0:T(1024)(128)(4,1)}), s8[4194304]{0:T(1024)(128)(4,1)S(1)}, s32[]{:S(2)}) async-start(s8[11010048]{0:T(1024)(128)(4,1)} %bitcast.16), calls=%async_computation.1 | async-start | bytes 8388608
  36.8 3.3 %slice-start.2 = ((s8[11010048]{0:T(1024)(128)(4,1)}), s8[2621440]{0:T(1024)(128)(4,1)S(1)}, s32[]{:S(2)}) async-start(s8[11010048]{0:T(1024)(128)(4,1)} %bitcast.16), calls=%async_computation.2 | async-start | bytes 5242880
  38.4 7.0 %copy-start.2 = (f32[1344]{0:T(1024)S(1)}, f32[1344]{0:T(1024)}, u32[]{:S(2)}) copy-start(f32[1344]{0:T(1024)} %param.25) | copy-start | bytes 16132
  38.4 11.9 %copy-start.1 = (bf16[8,5376]{1,0:T(8,128)(2,1)S(1)}, bf16[8,5376]{1,0:T(8,128)(2,1)}, u32[]{:S(2)}) copy-start(bf16[8,5376]{1,0:T(8,128)(2,1)} %refs_4_.3) | copy-start | bytes 258052
  41.8 4.5 %collective-permute-start.7 = (bf16[8,5376]{1,0:T(8,128)(2,1)S(1)}, bf16[8,5376]{1,0:T(8,128)(2,1)S(1)}, u32[]{:S(2)}, u32[]{:S(2)}) collective-permute-start(bf16[8,5376]{1,0:T(8,128)(2,1)S(1)} %get-tuple-element.49), channel_id=1, source_target_pairs={{0,1},{1,0},{2,3},{3,2},{4,5},{5,4},{6,7},{7,6},{8,9},{9,8},{10,11... | collective-permute-start | bytes 258056 | tf_op jit(solution)/shard_map/ppermute | solution.py:359
  43.4 5.4 %collective-permute-start.8 = (bf16[8,5376]{1,0:T(8,128)(2,1)S(1)}, bf16[8,5376]{1,0:T(8,128)(2,1)S(1)}, u32[]{:S(2)}, u32[]{:S(2)}) collective-permute-start(bf16[8,5376]{1,0:T(8,128)(2,1)S(1)} %get-tuple-element.49), channel_id=1, source_target_pairs={{0,2},{1,3},{2,0},{3,1},{4,6},{5,7},{6,4},{7,5},{8,10},{9,11},{10,... | collective-permute-start | bytes 258056 | tf_op jit(solution)/shard_map/ppermute | solution.py:359
  44.9 5.4 %collective-permute-start.9 = (bf16[8,5376]{1,0:T(8,128)(2,1)S(1)}, bf16[8,5376]{1,0:T(8,128)(2,1)S(1)}, u32[]{:S(2)}, u32[]{:S(2)}) collective-permute-start(bf16[8,5376]{1,0:T(8,128)(2,1)S(1)} %get-tuple-element.49), channel_id=1, source_target_pairs={{0,3},{1,2},{2,1},{3,0},{4,7},{5,6},{6,5},{7,4},{8,11},{9,10},{10,... | collective-permute-start | bytes 258056 | tf_op jit(solution)/shard_map/ppermute | solution.py:359
